TPU v7x, 32 devices: a whole 2x2x4 slice. The times are simulated.
32 devices in a mesh: groups: 2 (over x), seq: 16 (over z, y, core).
Axes of the slice: x: 2, y: 2, z: 4, core: 2. Of those that a mesh axis runs over, the one named last changes fastest.
Arguments:
- queries: bfloat16 [32, 32, 1024], P('seq', 'groups'), parts along dimension 1, may hold values from -1100 to 1100
- keys: bfloat16 [32, 32, 128], P('seq', 'groups'), parts along dimension 1, may hold values from -4 to 4
- values: bfloat16 [32, 32, 128], P('seq', 'groups'), parts along dimension 1, may hold values from -6 to 6
- cache_keys: bfloat16 [32, 2048, 128], P(('groups', 'seq')), parts along dimension 0, may hold values from -4 to 4
- cache_values: bfloat16 [32, 2048, 128], P(('groups', 'seq')), parts along dimension 0, may hold values from -6 to 6
- cache_len: int32 [32, 16], P(None, 'groups'), parts along dimension 1, may hold values from 1 to 2048, as said below
- out_weight: bfloat16 [2048, 2048], P('seq'), may hold values from -0.5 to 0.5
- norm_gain: bfloat16 [2048], replicated, may hold values from 0.5 to 1.5
- expert_ids: int32 [32, 16, 8], P('seq', 'groups'), parts along dimension 1, may hold values from 0 to 31, all different within a row; in each aligned block of 16 rows (0 to 15, 16 to 31, ..., all dimensions but the last counted through in order) at most 5 rows name the same one
- route_weights: float32 [32, 16, 8], P('seq', 'groups'), parts along dimension 1, may hold values from 0.02 to 1
- w_gate: bfloat16 [32, 2048, 384], P('seq'), may hold values from -0.125 to 0.125
- w_up: bfloat16 [32, 2048, 384], P('seq'), may hold values from -0.125 to 0.125
- w_down: bfloat16 [32, 384, 2048], P('seq'), may hold values from -0.3125 to 0.3125
Outputs:
- projected: bfloat16 [32, 16, 2048], P('seq', 'groups'), parts along dimension 1
- moe_out: bfloat16 [32, 16, 2048], P('seq', 'groups'), parts along dimension 1
There are 2 independent parts, one for each index of `groups`. A program takes and returns all parts, laid end to end along the dimension named above; an argument that names none is the same for every part. Nothing has to cross between parts.
Inputs may be any that keep to these rules, and one draw needn't show every extreme that they name: `cache_len`: every new token sees at least one cached key; some token sees all 2048. `expert_ids`: rows are taken position-major over members; in each aligned block of 16 rows (the rows of one index of seq) no expert is named more than 5 times, a bound that some block reaches.
All inputs are finite; a program needn't handle non-finite values.
Results may differ from a plain program's by a relative error of at most 0.01.
Values may be sent and summed in bfloat16 or wider, within the bound.
No kernel may reach another device: no remote copies, remote signals or barrier semaphores. Data moves between devices by JAX's collectives and lax.ppermute only.
A program may use at most 64 MiB of HBM per device.

v0:
```python
import jax
import jax.numpy as jnp
from jax import lax
from jax.sharding import PartitionSpec as P

D = 2048
HD = 128
TOPK = 8
QH = 16
KVH = 2
CAP = 5


def attend(query_heads, key_rows, value_rows, lengths):
    new_count = query_heads.shape[0]
    cache_count = key_rows.shape[0] - new_count
    scores = jnp.einsum(
        "qhd,kd->hqk", query_heads, key_rows, preferred_element_type=jnp.float32
    ) * HD ** (-0.5)
    cached_ok = jnp.arange(cache_count, dtype=jnp.int32)[None, :] < lengths[:, None]
    causal_ok = (
        jnp.arange(new_count, dtype=jnp.int32)[None, :]
        <= jnp.arange(new_count, dtype=jnp.int32)[:, None]
    )
    visible = jnp.concatenate([cached_ok, causal_ok], axis=1)
    scores = jnp.where(visible[None], scores, -1e30)
    row_max = jnp.max(scores, axis=-1, keepdims=True)
    expo = jnp.exp(scores - row_max)
    row_sum = jnp.sum(expo, axis=-1, keepdims=True)
    weights = (expo / row_sum).astype(jnp.bfloat16)
    result = jnp.einsum("hqk,kd->qhd", weights, value_rows, preferred_element_type=jnp.float32)
    return result.astype(jnp.bfloat16).reshape(new_count, -1)


def body(
    queries,
    keys,
    values,
    cache_keys,
    cache_values,
    cache_len,
    out_weight,
    norm_gain,
    expert_ids,
    route_weights,
    w_gate,
    w_up,
    w_down,
):
    slot_count = lax.axis_size("seq")
    per_rows = queries.shape[0]
    members = slot_count // KVH
    group_q = QH // KVH
    new_count = per_rows * slot_count
    position_index = lax.axis_index("seq")
    member = position_index // KVH
    query_rows, key_new, value_new = (
        lax.all_to_all(queries, "seq", split_axis=1, concat_axis=0, tiled=True),
        lax.all_to_all(keys, "seq", split_axis=1, concat_axis=0, tiled=True),
        lax.all_to_all(values, "seq", split_axis=1, concat_axis=0, tiled=True),
    )
    key_rows = jnp.concatenate([cache_keys[0], key_new.reshape(new_count, HD)], axis=0)
    value_rows = jnp.concatenate([cache_values[0], value_new.reshape(new_count, HD)], axis=0)
    lengths = lax.dynamic_slice_in_dim(cache_len, member, 1, 1)[:, 0]
    attended = attend(query_rows.reshape(new_count, group_q, HD), key_rows, value_rows, lengths)
    returned_heads = lax.all_to_all(
        attended[:, None, :], "seq", split_axis=0, concat_axis=1, tiled=True
    )
    token_heads = returned_heads.reshape(per_rows * members, QH * HD)
    projected_f = jnp.dot(
        token_heads,
        lax.all_gather(out_weight, "seq", axis=0, tiled=True),
        preferred_element_type=jnp.float32,
    )
    projected_f = projected_f.reshape(per_rows, members, D)
    projected = projected_f.astype(jnp.bfloat16)
    token_count = per_rows * members
    flat_rows = projected.reshape(token_count, D).astype(jnp.float32)
    stats = jnp.mean(flat_rows * flat_rows, axis=-1, keepdims=True)
    normed = (flat_rows * lax.rsqrt(stats + 1e-06) * norm_gain.astype(jnp.float32)).astype(
        jnp.bfloat16
    )
    exp_dev = w_gate.shape[0]
    expert_count = exp_dev * slot_count
    chosen_ids = expert_ids.reshape(token_count * TOPK)
    onehot = (chosen_ids[:, None] == jnp.arange(expert_count, dtype=jnp.int32)[None, :]).astype(
        jnp.int32
    )
    slot_rank = jnp.sum((jnp.cumsum(onehot, axis=0) - onehot) * onehot, axis=1)
    owner = chosen_ids // exp_dev
    local_expert = chosen_ids % exp_dev
    slot_target = (local_expert * slot_count + owner) * CAP + slot_rank
    total_slots = exp_dev * slot_count * CAP
    token_of = jnp.arange(token_count * TOPK, dtype=jnp.int32) // TOPK
    source_row = jnp.full((total_slots,), -1, jnp.int32).at[slot_target].set(token_of)
    filled = source_row >= 0
    outgoing = jnp.where(
        filled[:, None], normed[jnp.maximum(source_row, 0)], jnp.zeros((), jnp.bfloat16)
    )
    outgoing = outgoing.reshape(exp_dev, slot_count, CAP, D)
    incoming = lax.all_to_all(outgoing, "seq", split_axis=1, concat_axis=1, tiled=True)
    row_block = incoming.reshape(exp_dev, slot_count * CAP, D)
    gate_out = jnp.einsum("ecd,edf->ecf", row_block, w_gate, preferred_element_type=jnp.float32)
    up_out = jnp.einsum("ecd,edf->ecf", row_block, w_up, preferred_element_type=jnp.float32)
    hidden_act = (jax.nn.silu(gate_out) * up_out).astype(jnp.bfloat16)
    expert_out = jnp.einsum(
        "ecf,efd->ecd", hidden_act, w_down, preferred_element_type=jnp.float32
    ).astype(jnp.bfloat16)
    expert_back = lax.all_to_all(
        expert_out.reshape(exp_dev, slot_count, CAP, D),
        "seq",
        split_axis=1,
        concat_axis=1,
        tiled=True,
    )
    picked = expert_back.reshape(total_slots, D)[slot_target].reshape(token_count, TOPK, D)
    raw_weights = route_weights.reshape(token_count, TOPK)
    norm_weights = raw_weights / jnp.sum(raw_weights, axis=1, keepdims=True)
    mixed = jnp.sum(norm_weights[:, :, None] * picked.astype(jnp.float32), axis=1)
    moe_out = mixed.astype(jnp.bfloat16).reshape(per_rows, members, D)
    return (projected, moe_out)


def solution(mesh):
    return jax.shard_map(
        body,
        mesh=mesh,
        in_specs=(
            P("seq", "groups", None),
            P("seq", "groups", None),
            P("seq", "groups", None),
            P(("groups", "seq"), None, None),
            P(("groups", "seq"), None, None),
            P(None, "groups"),
            P("seq", None),
            P(),
            P("seq", "groups", None),
            P("seq", "groups", None),
            P("seq", None, None),
            P("seq", None, None),
            P("seq", None, None),
        ),
        out_specs=(P("seq", "groups", None), P("seq", "groups", None)),
        check_vma=False,
    )
```

profile of v0, /device:TPU:0, one launch (start us, length us, event | category | flops | bytes accessed | tf_op | source)
XLA Modules:
  0.0 167.0 jit_solution(5124968312826070863)
XLA Ops:
  7.9 1.7 %copy.33 = bf16[2,16,1024]{2,0,1:T(2,128)(2,1)} copy(bf16[2,16,1024]{2,1,0:T(8,128)(2,1)} %param.13) | data formatting | bytes 131072 | tf_op args[0]
  9.7 7.4 %all-to-all-start.2 = ((bf16[2,16,1024]{2,0,1:T(2,128)(2,1)}), bf16[2,16,1024]{2,0,1:T(2,128)(2,1)S(1)}, u32[]{:S(2)}, u32[]{:S(2)}) async-start(bf16[2,16,1024]{2,0,1:T(2,128)(2,1)} %copy.33), calls=%async_computation.2 | async-start | bytes 131072 | tf_op jit(solution)/shard_map/all_to_all | solution.py:58
  22.3 1.7 %all-to-all-done.2 = bf16[2,16,1024]{2,0,1:T(2,128)(2,1)S(1)} async-done(((bf16[2,16,1024]{2,0,1:T(2,128)(2,1)}), bf16[2,16,1024]{2,0,1:T(2,128)(2,1)S(1)}, u32[]{:S(2)}, u32[]{:S(2)}) %all-to-all-start.2) | async-done | bytes 65568 | tf_op jit(solution)/shard_map/all_to_all | solution.py:58
  24.0 4.3 %all-to-all-start.1 = ((bf16[2,16,128]{2,0,1:T(2,128)(2,1)}), bf16[2,16,128]{2,0,1:T(2,128)(2,1)S(1)}, u32[]{:S(2)}, u32[]{:S(2)}) async-start(bf16[2,16,128]{2,0,1:T(2,128)(2,1)} %copy.32), calls=%async_computation.1 | async-start | bytes 16384 | tf_op jit(solution)/shard_map/all_to_all | solution.py:59
  29.7 5.3 %all-to-all-done.1 = bf16[2,16,128]{2,0,1:T(2,128)(2,1)S(1)} async-done(((bf16[2,16,128]{2,0,1:T(2,128)(2,1)}), bf16[2,16,128]{2,0,1:T(2,128)(2,1)S(1)}, u32[]{:S(2)}, u32[]{:S(2)}) %all-to-all-start.1) | async-done | bytes 8224 | tf_op jit(solution)/shard_map/all_to_all | solution.py:59
  34.9 3.5 %all-to-all-start = ((bf16[2,16,128]{2,0,1:T(2,128)(2,1)}), bf16[2,16,128]{2,0,1:T(2,128)(2,1)S(1)}, u32[]{:S(2)}, u32[]{:S(2)}) async-start(bf16[2,16,128]{2,0,1:T(2,128)(2,1)} %copy.31), calls=%async_computation | async-start | bytes 16384 | tf_op jit(solution)/shard_map/all_to_all | solution.py:60
  38.4 3.4 %fusion.50 = (f32[8,32]{1,0:T(8,128)S(1)}, f32[8,32,2080]{2,1,0:T(8,128)}) fusion(pred[32,2080]{1,0:T(8,128)(4,1)S(1)} %pad_add_fusion, bf16[32,128]{1,0:T(8,128)(2,1)S(1)} %bitcast.89, bf16[2048,128]{1,0:T(8,128)(2,1)} %bitcast.91, bf16[32,8,128]{2,1,0:T(8,128)(2,1)S(1)} %reshape.222), kind=kOutput, calls=%fused_computation.81 | convolution fusion | flops 139511840 | bytes 2795520 | tf_op jit(solution)/shard_map/sub | solution.py:28
  41.8 2.9 %all-to-all-done = bf16[2,16,128]{2,0,1:T(2,128)(2,1)S(1)} async-done(((bf16[2,16,128]{2,0,1:T(2,128)(2,1)}), bf16[2,16,128]{2,0,1:T(2,128)(2,1)S(1)}, u32[]{:S(2)}, u32[]{:S(2)}) %all-to-all-start) | async-done | bytes 8224 | tf_op jit(solution)/shard_map/all_to_all | solution.py:60
  44.7 2.3 %fusion.11 = bf16[32,8,128]{2,0,1:T(8,128)(2,1)S(1)} fusion(f32[8,32,2080]{2,1,0:T(8,128)} %get-tuple-element.3, f32[8,32]{1,0:T(8,128)S(1)} %get-tuple-element.2, bf16[32,128]{1,0:T(8,128)(2,1)S(1)} %bitcast.90, bf16[2048,128]{1,0:T(8,128)(2,1)} %bitcast.92), kind=kOutput, calls=%fused_computation.17 | convolution fusion | flops 138477568 | bytes 2728960 | tf_op jit(solution)/shard_map/hqk,kd->qhd/dot_general | solution.py:31
  49.3 3.5 %all-to-all-start.3 = ((bf16[16,2,1024]{2,1,0:T(2,128)(2,1)}), bf16[16,2,1024]{2,1,0:T(2,128)(2,1)S(1)}, u32[]{:S(2)}, u32[]{:S(2)}) async-start(bf16[16,2,1024]{2,1,0:T(2,128)(2,1)} %reshape.261), calls=%async_computation.3 | async-start | bytes 131072 | tf_op jit(solution)/shard_map/all_to_all | solution.py:66
  53.0 8.1 %all-to-all-done.3 = bf16[16,2,1024]{2,1,0:T(2,128)(2,1)S(1)} async-done(((bf16[16,2,1024]{2,1,0:T(2,128)(2,1)}), bf16[16,2,1024]{2,1,0:T(2,128)(2,1)S(1)}, u32[]{:S(2)}, u32[]{:S(2)}) %all-to-all-start.3) | async-done | bytes 65568 | tf_op jit(solution)/shard_map/all_to_all | solution.py:66
  61.6 26.4 %all-gather.2.cloned.1.call-done = bf16[2048,2048]{1,0:T(8,128)(2,1)} async-done(((bf16[128,2048]{1,0:T(8,128)(2,1)}), bf16[2048,2048]{1,0:T(8,128)(2,1)}) %all-gather.2.cloned.1.call-update) | async-done | bytes 8388624 | tf_op jit(solution)/shard_map/all_gather | solution.py:72
  88.0 4.7 %fusion.29 = (f32[2,8]{1,0:T(2,128)S(1)}, bf16[2,8,2048]{2,1,0:T(8,128)(2,1)S(1)}) fusion(bf16[2,8,2048]{2,1,0:T(8,128)(2,1)S(1)} %dot_general.22, bf16[2048,2048]{1,0:T(8,128)(2,1)} %all-gather.2.cloned.1.call-done), kind=kOutput, calls=%fused_computation.42 | convolution fusion | flops 134348784 | bytes 8519744 | tf_op jit(solution)/shard_map/dot_general | solution.py:70
  92.9 1.9 %gather_fusion = bf16[160,2048]{1,0:T(8,128)(2,1)} fusion(bf16[16,2048]{1,0:T(8,128)(2,1)S(1)} %fusion.28, s32[1024]{0:T(1024)S(1)} %pad_clamp_fusion.1), kind=kCustom, calls=%fused_computation | custom fusion | bytes 1311360 | tf_op jit(solution)/shard_map/gather | solution.py:98
  94.8 2.2 %gather.9 = bf16[2,16,5,2048]{3,2,1,0:T(8,128)(2,1)} reshape(bf16[160,2048]{1,0:T(8,128)(2,1)} %gather_fusion) | data formatting | bytes 1310720 | tf_op jit(solution)/shard_map/gather | solution.py:98
  99.3 21.4 %all_to_all.70 = bf16[2,16,5,2048]{3,0,2,1:T(2,128)(2,1)S(1)} all-to-all(bf16[2,16,5,2048]{3,0,2,1:T(2,128)(2,1)S(1)} %copy.40), channel_id=1, replica_groups=mesh['groups'=2,'seq'=16] {'seq'}, dimensions={1} | all-to-all | bytes 1310720 | tf_op jit(solution)/shard_map/all_to_all | solution.py:101
  122.3 4.3 %convolution_convert_fusion = bf16[2,80,2048]{2,1,0:T(8,128)(2,1)} fusion(bf16[2,384,2048]{2,1,0:T(8,128)(2,1)S(1)} %copy-done, bf16[2,2048,384]{2,1,0:T(8,128)(2,1)} %param.24, bf16[2,80,2048]{2,0,1:T(2,128)(2,1)} %bitcast.83, f32[2,80,384]{2,1,0:T(8,128)S(1)} %fusion.15), kind=kOutput, calls=%fused_computation.11 | convolution fusion | flops 504012800 | bytes 7847936 | tf_op jit(solution)/shard_map/ecf,efd->ecd/dot_general | solution.py:106
  126.6 2.6 %copy.43 = bf16[2,80,2048]{2,0,1:T(2,128)(2,1)} copy(bf16[2,80,2048]{2,1,0:T(8,128)(2,1)} %convolution_convert_fusion) | data formatting | bytes 1310720 | tf_op jit(solution)/shard_map/convert_element_type | solution.py:108
  129.2 4.3 %all-to-all-start.5 = ((bf16[2,16,5,2048]{3,0,2,1:T(2,128)(2,1)}), bf16[2,16,5,2048]{3,0,2,1:T(2,128)(2,1)}, u32[]{:S(2)}, u32[]{:S(2)}) async-start(bf16[2,16,5,2048]{3,0,2,1:T(2,128)(2,1)} %bitcast.84), calls=%async_computation.5 | async-start | bytes 1310720 | tf_op jit(solution)/shard_map/all_to_all | solution.py:109
  133.8 16.2 %all-to-all-done.5 = bf16[2,16,5,2048]{3,0,2,1:T(2,128)(2,1)} async-done(((bf16[2,16,5,2048]{3,0,2,1:T(2,128)(2,1)}), bf16[2,16,5,2048]{3,0,2,1:T(2,128)(2,1)}, u32[]{:S(2)}, u32[]{:S(2)}) %all-to-all-start.5) | async-done | bytes 655392 | tf_op jit(solution)/shard_map/all_to_all | solution.py:109
  150.1 2.4 %copy.44 = bf16[2,16,5,2048]{3,2,1,0:T(8,128)(2,1)} copy(bf16[2,16,5,2048]{3,0,2,1:T(2,128)(2,1)} %all-to-all-done.5) | data formatting | bytes 1310720 | tf_op jit(solution)/shard_map/all_to_all | solution.py:109
  152.4 2.2 %reshape.227 = bf16[160,2048]{1,0:T(8,128)(2,1)} reshape(bf16[2,16,5,2048]{3,2,1,0:T(8,128)(2,1)} %copy.44) | data formatting | bytes 1310720 | tf_op jit(solution)/shard_map/reshape | solution.py:116
  154.6 3.4 %gather_fusion.1 = bf16[128,2048]{1,0:T(8,128)(2,1)} fusion(bf16[160,2048]{1,0:T(8,128)(2,1)} %reshape.227, s32[1024]{0:T(1024)S(1)} %pad_clamp_fusion), kind=kCustom, calls=%fused_computation.1 | custom fusion | bytes 1049088 | tf_op jit(solution)/shard_map/gather | solution.py:116
  158.0 2.1 %fusion.12 = bf16[16,2048]{1,0:T(8,128)(2,1)} fusion(bf16[128,2048]{1,0:T(8,128)(2,1)} %gather_fusion.1, f32[16,8]{1,0:T(8,128)S(1)} %copy.39), kind=kLoop, calls=%fused_computation.19 | loop fusion | flops 753664 | bytes 590336 | tf_op jit(solution)/shard_map/reduce_sum | solution.py:119
  (56 shorter events, 14.5 us)
Async XLA Ops:
  7.2 115.2 %copy-start = (bf16[2,384,2048]{2,1,0:T(8,128)(2,1)S(1)}, bf16[2,384,2048]{2,1,0:T(8,128)(2,1)}, u32[]{:S(2)}) copy-start(bf16[2,384,2048]{2,1,0:T(8,128)(2,1)} %param.25) | copy-start | bytes 9437188
  7.2 80.9 %all-gather.2.cloned.1.call-start = ((), (), s32[]{:S(2)}) async-start(), calls=%async_computation.6 | async-start | bytes 8912896 | tf_op jit(solution)/shard_map/all_gather | solution.py:72
  9.7 14.3 %all-to-all-start.2 = ((bf16[2,16,1024]{2,0,1:T(2,128)(2,1)}), bf16[2,16,1024]{2,0,1:T(2,128)(2,1)S(1)}, u32[]{:S(2)}, u32[]{:S(2)}) async-start(bf16[2,16,1024]{2,0,1:T(2,128)(2,1)} %copy.33), calls=%async_computation.2 | async-start | bytes 131072 | tf_op jit(solution)/shard_map/all_to_all | solution.py:58
  24.0 10.9 %all-to-all-start.1 = ((bf16[2,16,128]{2,0,1:T(2,128)(2,1)}), bf16[2,16,128]{2,0,1:T(2,128)(2,1)S(1)}, u32[]{:S(2)}, u32[]{:S(2)}) async-start(bf16[2,16,128]{2,0,1:T(2,128)(2,1)} %copy.32), calls=%async_computation.1 | async-start | bytes 16384 | tf_op jit(solution)/shard_map/all_to_all | solution.py:59
  34.9 9.8 %all-to-all-start = ((bf16[2,16,128]{2,0,1:T(2,128)(2,1)}), bf16[2,16,128]{2,0,1:T(2,128)(2,1)S(1)}, u32[]{:S(2)}, u32[]{:S(2)}) async-start(bf16[2,16,128]{2,0,1:T(2,128)(2,1)} %copy.31), calls=%async_computation | async-start | bytes 16384 | tf_op jit(solution)/shard_map/all_to_all | solution.py:60
  44.7 8.1 %copy-start.5 = (bf16[2048]{0:T(1024)(128)(2,1)S(1)}, bf16[2048]{0:T(1024)(128)(2,1)}, u32[]{:S(2)}) copy-start(bf16[2048]{0:T(1024)(128)(2,1)} %param.20) | copy-start | bytes 12292
  49.3 11.8 %all-to-all-start.3 = ((bf16[16,2,1024]{2,1,0:T(2,128)(2,1)}), bf16[16,2,1024]{2,1,0:T(2,128)(2,1)S(1)}, u32[]{:S(2)}, u32[]{:S(2)}) async-start(bf16[16,2,1024]{2,1,0:T(2,128)(2,1)} %reshape.261), calls=%async_computation.3 | async-start | bytes 131072 | tf_op jit(solution)/shard_map/all_to_all | solution.py:66
  92.7 2.1 %copy-start.3 = (bf16[2,8,2048]{2,1,0:T(8,128)(2,1)}, bf16[2,8,2048]{2,1,0:T(8,128)(2,1)S(1)}, u32[]{:S(2)}) copy-start(bf16[2,8,2048]{2,1,0:T(8,128)(2,1)S(1)} %get-tuple-element.5) | copy-start | bytes 196612
  97.0 24.5 %copy-start.2 = (bf16[2,2048,384]{2,1,0:T(8,128)(2,1)S(1)}, bf16[2,2048,384]{2,1,0:T(8,128)(2,1)}, u32[]{:S(2)}) copy-start(bf16[2,2048,384]{2,1,0:T(8,128)(2,1)} %param.23) | copy-start | bytes 9437188
  120.7 0.9 copy-start.1
  126.6 6.9 %copy-start.4 = (f32[2,8,8]{2,1,0:T(8,128)S(1)}, f32[2,8,8]{2,1,0:T(8,128)}, u32[]{:S(2)}) copy-start(f32[2,8,8]{2,1,0:T(8,128)} %param.22) | copy-start | bytes 1540
  129.2 20.9 %all-to-all-start.5 = ((bf16[2,16,5,2048]{3,0,2,1:T(2,128)(2,1)}), bf16[2,16,5,2048]{3,0,2,1:T(2,128)(2,1)}, u32[]{:S(2)}, u32[]{:S(2)}) async-start(bf16[2,16,5,2048]{3,0,2,1:T(2,128)(2,1)} %bitcast.84), calls=%async_computation.5 | async-start | bytes 1310720 | tf_op jit(solution)/shard_map/all_to_all | solution.py:109
Sparse Core Ops, SparseCore 0:
  10.2 77.8 all-gather.1
where the time goes:
time: 168 us; the launch traced here: 167 us
  waiting for transfers between devices  61.4 us (37%)
  local copies, waits for them, and re-layouts  25.7 us (15%)
  starting transfers between devices  23 us (14%)
  blocking collectives  21.4 us (13%)
  matrix products  15.4 us (9%)
  between operations  14.3 us (9%)
  other arithmetic  5.82 us (3%)
    all_gather x1, waiting for transfers between devices, body(): lax.all_gather(out_weight, 'seq', axis=0, tiled=True)  26.4 us
    all_to_all x1, blocking collectives, body(): lax.all_to_all(outgoing, 'seq', split_axis=1, concat_axis=1, tiled=True)  21.4 us
    all_to_all x1, waiting for transfers between devices, body(): lax.all_to_all(expert_out.reshape(exp_dev, slot_count, CAP, D), 'seq', sp...  16.2 us
    all_to_all x1, waiting for transfers between devices, body(): lax.all_to_all(attended[:, None, :], 'seq', split_axis=0, concat_axis=1,...  8.13 us
    all_to_all x1, starting transfers between devices, body(): lax.all_to_all(queries, 'seq', split_axis=1, concat_axis=0, tiled=True)  7.41 us
    unnamed x17, local copies, waits for them, and re-layouts  5.94 us
    all_to_all x1, waiting for transfers between devices, body(): lax.all_to_all(keys, 'seq', split_axis=1, concat_axis=0, tiled=True)  5.26 us
    dot_general x1, matrix products, body(): jnp.dot(token_heads, lax.all_gather(out_weight, 'seq', axis=0, tiled=True...  4.66 us
  transfers between devices with their start and end apart: 6, of which 6 were waited for; matrix products, arithmetic and copies ran while one was open for 10% of the time, Pallas kernels for 0%

commit v1 on v0

--- a/solution.py
+++ b/solution.py
@@ -9,6 +9,11 @@
 QH = 16
 KVH = 2
 CAP = 5
+
+
+def all_by_exchange(x, axis, dim):
+    outgoing = jnp.stack([x] * lax.axis_size(axis))
+    return jnp.concatenate(lax.all_to_all(outgoing, axis, 0, 0), axis=dim)
 
 
 def attend(query_heads, key_rows, value_rows, lengths):
@@ -68,9 +73,7 @@
     )
     token_heads = returned_heads.reshape(per_rows * members, QH * HD)
     projected_f = jnp.dot(
-        token_heads,
-        lax.all_gather(out_weight, "seq", axis=0, tiled=True),
-        preferred_element_type=jnp.float32,
+        token_heads, all_by_exchange(out_weight, "seq", 0), preferred_element_type=jnp.float32
     )
     projected_f = projected_f.reshape(per_rows, members, D)
     projected = projected_f.astype(jnp.bfloat16)

time: 168 us -> 317 us (1.89)
  waiting for transfers between devices: 61.4 us -> 177 us
  blocking collectives: 21.4 us -> 64.3 us
  between operations: 14.3 us -> 0.93 us
  local copies, waits for them, and re-layouts: 25.7 us -> 29 us
    all_to_all x1, waiting for transfers between devices: 8.13 us -> 148 us  [all_by_exchange(): return jnp.concatenate(lax.all_to_all(outgoing, axis, 0, 0), axis=dim)]
    all_to_all x1, blocking collectives: 21.4 us -> 54.5 us  [body(): lax.all_to_all(outgoing, 'seq', split_axis=1, concat_axis=1, tiled=True)]
    all_gather x1 -> x0, waiting for transfers between devices: 26.4 us -> none  [body(): lax.all_gather(out_weight, 'seq', axis=0, tiled=True)]
    all_to_all x0 -> x1, blocking collectives: none -> 9.74 us  [body(): lax.all_to_all(attended[:, None, :], 'seq', split_axis=0, concat_axis=1,...]
    another operation x0 -> x1, local copies, waits for them, and re-layouts: none -> 5.32 us  [all_by_exchange(): outgoing = jnp.stack([x] * lax.axis_size(axis))]
  transfers between devices with their start and end apart: 6 -> 5, of which waited for: 6 -> 5; matrix products, arithmetic and copies ran while one was open for 10% -> 3% of each run, Pallas kernels for 0% -> 0%
where the time goes in v1:
time: 317 us; the launch traced here: 316 us
  waiting for transfers between devices  177 us (56%)
  blocking collectives  64.3 us (20%)
  local copies, waits for them, and re-layouts  29 us (9%)
  starting transfers between devices  23.5 us (7%)
  matrix products  15.4 us (5%)
  other arithmetic  5.81 us (2%)
    all_to_all x1, waiting for transfers between devices, all_by_exchange(): return jnp.concatenate(lax.all_to_all(outgoing, axis, 0, 0), axis=dim)  148 us
    all_to_all x1, blocking collectives, body(): lax.all_to_all(outgoing, 'seq', split_axis=1, concat_axis=1, tiled=True)  54.5 us
    all_to_all x1, waiting for transfers between devices, body(): lax.all_to_all(expert_out.reshape(exp_dev, slot_count, CAP, D), 'seq', sp...  16.2 us
    all_to_all x1, blocking collectives, body(): lax.all_to_all(attended[:, None, :], 'seq', split_axis=0, concat_axis=1,...  9.74 us
    all_to_all x1, starting transfers between devices, body(): lax.all_to_all(queries, 'seq', split_axis=1, concat_axis=0, tiled=True)  7.41 us
  transfers between devices with their start and end apart: 5, of which 5 were waited for; matrix products, arithmetic and copies ran while one was open for 3% of the time, Pallas kernels for 0%

profile of v1, /device:TPU:0, one launch (start us, length us, event | category | flops | bytes accessed | tf_op | source)
XLA Modules:
  0.0 315.9 jit_solution(10542408048876071085)
XLA Ops:
  2.3 7.4 %all-to-all-start.2 = ((bf16[2,16,1024]{2,0,1:T(2,128)(2,1)}), bf16[2,16,1024]{2,0,1:T(2,128)(2,1)S(1)}, u32[]{:S(2)}, u32[]{:S(2)}) async-start(bf16[2,16,1024]{2,0,1:T(2,128)(2,1)} %copy.33), calls=%async_computation.2 | async-start | bytes 131072 | tf_op jit(solution)/shard_map/all_to_all | solution.py:63
  11.9 4.8 %all-to-all-done.2 = bf16[2,16,1024]{2,0,1:T(2,128)(2,1)S(1)} async-done(((bf16[2,16,1024]{2,0,1:T(2,128)(2,1)}), bf16[2,16,1024]{2,0,1:T(2,128)(2,1)S(1)}, u32[]{:S(2)}, u32[]{:S(2)}) %all-to-all-start.2) | async-done | bytes 65568 | tf_op jit(solution)/shard_map/all_to_all | solution.py:63
  16.7 3.5 %all-to-all-start.1 = ((bf16[2,16,128]{2,0,1:T(2,128)(2,1)}), bf16[2,16,128]{2,0,1:T(2,128)(2,1)S(1)}, u32[]{:S(2)}, u32[]{:S(2)}) async-start(bf16[2,16,128]{2,0,1:T(2,128)(2,1)} %copy.32), calls=%async_computation.1 | async-start | bytes 16384 | tf_op jit(solution)/shard_map/all_to_all | solution.py:64
  21.5 5.0 %all-to-all-done.1 = bf16[2,16,128]{2,0,1:T(2,128)(2,1)S(1)} async-done(((bf16[2,16,128]{2,0,1:T(2,128)(2,1)}), bf16[2,16,128]{2,0,1:T(2,128)(2,1)S(1)}, u32[]{:S(2)}, u32[]{:S(2)}) %all-to-all-start.1) | async-done | bytes 8224 | tf_op jit(solution)/shard_map/all_to_all | solution.py:64
  26.5 3.5 %all-to-all-start = ((bf16[2,16,128]{2,0,1:T(2,128)(2,1)}), bf16[2,16,128]{2,0,1:T(2,128)(2,1)S(1)}, u32[]{:S(2)}, u32[]{:S(2)}) async-start(bf16[2,16,128]{2,0,1:T(2,128)(2,1)} %copy.31), calls=%async_computation | async-start | bytes 16384 | tf_op jit(solution)/shard_map/all_to_all | solution.py:65
  29.9 3.4 %fusion.45 = (f32[8,32]{1,0:T(8,128)S(1)}, f32[8,32,2080]{2,1,0:T(8,128)}) fusion(pred[32,2080]{1,0:T(8,128)(4,1)S(1)} %pad_add_fusion, bf16[32,128]{1,0:T(8,128)(2,1)S(1)} %bitcast.86, bf16[2048,128]{1,0:T(8,128)(2,1)} %bitcast.88, bf16[32,8,128]{2,1,0:T(8,128)(2,1)S(1)} %reshape.227), kind=kOutput, calls=%fused_computation.79 | convolution fusion | flops 139511840 | bytes 2795520 | tf_op jit(solution)/shard_map/sub | solution.py:33
  33.3 2.9 all-to-all-done
  36.3 2.3 fusion.6
  40.2 9.7 %all_to_all.75 = bf16[16,2,1024]{2,1,0:T(2,128)(2,1)S(1)} all-to-all(bf16[16,2,1024]{2,1,0:T(2,128)(2,1)S(1)} %reshape.267), channel_id=1, replica_groups=mesh['groups'=2,'seq'=16] {'seq'}, dimensions={0} | all-to-all | bytes 131072 | tf_op jit(solution)/shard_map/all_to_all | solution.py:71
  49.9 5.3 %stack.2 = bf16[16,128,2048]{2,1,0:T(8,128)(2,1)} broadcast(bf16[128,2048]{1,0:T(8,128)(2,1)} %param.19), dimensions={1,2} | broadcast | bytes 8912896 | tf_op jit(solution)/shard_map/stack | solution.py:15
  55.3 4.9 %all-to-all-start.4 = ((bf16[16,128,2048]{2,1,0:T(8,128)(2,1)}), bf16[16,128,2048]{2,1,0:T(8,128)(2,1)}, u32[]{:S(2)}, u32[]{:S(2)}) async-start(bf16[16,128,2048]{2,1,0:T(8,128)(2,1)} %stack.2), calls=%async_computation.4 | async-start | bytes 16777216 | tf_op jit(solution)/shard_map/all_to_all | solution.py:16
  62.5 148.2 %all-to-all-done.4 = bf16[16,128,2048]{2,1,0:T(8,128)(2,1)} async-done(((bf16[16,128,2048]{2,1,0:T(8,128)(2,1)}), bf16[16,128,2048]{2,1,0:T(8,128)(2,1)}, u32[]{:S(2)}, u32[]{:S(2)}) %all-to-all-start.4) | async-done | bytes 8388640 | tf_op jit(solution)/shard_map/all_to_all | solution.py:16
  210.6 4.7 %fusion.24 = (f32[2,8]{1,0:T(2,128)S(1)}, bf16[2,8,2048]{2,1,0:T(8,128)(2,1)S(1)}) fusion(bf16[2,8,2048]{2,1,0:T(8,128)(2,1)S(1)} %dot_general.22, bf16[2048,2048,1]{1,0,2:T(8,128)(2,1)} %bitcast.17), kind=kOutput, calls=%fused_computation.40 | convolution fusion | flops 134348784 | bytes 8519744 | tf_op jit(solution)/shard_map/dot_general | solution.py:75
  215.5 1.9 gather_fusion
  217.4 2.2 gather.9
  221.9 54.5 %all_to_all.76 = bf16[2,16,5,2048]{3,0,2,1:T(2,128)(2,1)S(1)} all-to-all(bf16[2,16,5,2048]{3,0,2,1:T(2,128)(2,1)S(1)} %copy.40), channel_id=1, replica_groups=mesh['groups'=2,'seq'=16] {'seq'}, dimensions={1} | all-to-all | bytes 1310720 | tf_op jit(solution)/shard_map/all_to_all | solution.py:104
  278.1 4.2 %convolution_convert_fusion = bf16[2,80,2048]{2,1,0:T(8,128)(2,1)} fusion(bf16[2,384,2048]{2,1,0:T(8,128)(2,1)S(1)} %copy-done, bf16[2,2048,384]{2,1,0:T(8,128)(2,1)} %param.24, bf16[2,80,2048]{2,0,1:T(2,128)(2,1)} %bitcast.80, f32[2,80,384]{2,1,0:T(8,128)S(1)} %fusion.10), kind=kOutput, calls=%fused_computation.9 | convolution fusion | flops 504012800 | bytes 7847936 | tf_op jit(solution)/shard_map/ecf,efd->ecd/dot_general | solution.py:109
  282.4 2.6 copy.43
  285.0 4.3 %all-to-all-start.6 = ((bf16[2,16,5,2048]{3,0,2,1:T(2,128)(2,1)}), bf16[2,16,5,2048]{3,0,2,1:T(2,128)(2,1)}, u32[]{:S(2)}, u32[]{:S(2)}) async-start(bf16[2,16,5,2048]{3,0,2,1:T(2,128)(2,1)} %bitcast.81), calls=%async_computation.6 | async-start | bytes 1310720 | tf_op jit(solution)/shard_map/all_to_all | solution.py:112
  289.6 16.2 %all-to-all-done.6 = bf16[2,16,5,2048]{3,0,2,1:T(2,128)(2,1)} async-done(((bf16[2,16,5,2048]{3,0,2,1:T(2,128)(2,1)}), bf16[2,16,5,2048]{3,0,2,1:T(2,128)(2,1)}, u32[]{:S(2)}, u32[]{:S(2)}) %all-to-all-start.6) | async-done | bytes 655392 | tf_op jit(solution)/shard_map/all_to_all | solution.py:112
  305.8 2.4 copy.44
  308.2 2.2 reshape.233
  310.4 3.4 %gather_fusion.1 = bf16[128,2048]{1,0:T(8,128)(2,1)} fusion(bf16[160,2048]{1,0:T(8,128)(2,1)} %reshape.233, s32[1024]{0:T(1024)S(1)} %pad_clamp_fusion), kind=kCustom, calls=%fused_computation.1 | custom fusion | bytes 1049088 | tf_op jit(solution)/shard_map/gather | solution.py:119
  313.8 2.1 fusion.7
  (57 shorter events, 13.4 us)
Async XLA Ops:
  0.6 277.5 %copy-start = (bf16[2,384,2048]{2,1,0:T(8,128)(2,1)S(1)}, bf16[2,384,2048]{2,1,0:T(8,128)(2,1)}, u32[]{:S(2)}) copy-start(bf16[2,384,2048]{2,1,0:T(8,128)(2,1)} %param.25) | copy-start | bytes 9437188
  2.3 14.3 %all-to-all-start.2 = ((bf16[2,16,1024]{2,0,1:T(2,128)(2,1)}), bf16[2,16,1024]{2,0,1:T(2,128)(2,1)S(1)}, u32[]{:S(2)}, u32[]{:S(2)}) async-start(bf16[2,16,1024]{2,0,1:T(2,128)(2,1)} %copy.33), calls=%async_computation.2 | async-start | bytes 131072 | tf_op jit(solution)/shard_map/all_to_all | solution.py:63
  16.7 9.8 %all-to-all-start.1 = ((bf16[2,16,128]{2,0,1:T(2,128)(2,1)}), bf16[2,16,128]{2,0,1:T(2,128)(2,1)S(1)}, u32[]{:S(2)}, u32[]{:S(2)}) async-start(bf16[2,16,128]{2,0,1:T(2,128)(2,1)} %copy.32), calls=%async_computation.1 | async-start | bytes 16384 | tf_op jit(solution)/shard_map/all_to_all | solution.py:64
  26.5 9.8 %all-to-all-start = ((bf16[2,16,128]{2,0,1:T(2,128)(2,1)}), bf16[2,16,128]{2,0,1:T(2,128)(2,1)S(1)}, u32[]{:S(2)}, u32[]{:S(2)}) async-start(bf16[2,16,128]{2,0,1:T(2,128)(2,1)} %copy.31), calls=%async_computation | async-start | bytes 16384 | tf_op jit(solution)/shard_map/all_to_all | solution.py:65
  55.3 4.9 %copy-start.5 = (s32[2,8,8]{2,1,0:T(8,128)S(1)}, s32[2,8,8]{2,1,0:T(8,128)}, u32[]{:S(2)}) copy-start(s32[2,8,8]{2,1,0:T(8,128)} %param.21) | copy-start | bytes 1540
  55.3 5.1 %copy-start.6 = (bf16[2048]{0:T(1024)(128)(2,1)S(1)}, bf16[2048]{0:T(1024)(128)(2,1)}, u32[]{:S(2)}) copy-start(bf16[2048]{0:T(1024)(128)(2,1)} %param.20) | copy-start | bytes 12292
  55.3 155.4 %all-to-all-start.4 = ((bf16[16,128,2048]{2,1,0:T(8,128)(2,1)}), bf16[16,128,2048]{2,1,0:T(8,128)(2,1)}, u32[]{:S(2)}, u32[]{:S(2)}) async-start(bf16[16,128,2048]{2,1,0:T(8,128)(2,1)} %stack.2), calls=%async_computation.4 | async-start | bytes 16777216 | tf_op jit(solution)/shard_map/all_to_all | solution.py:16
  215.3 2.1 copy-start.3
  219.6 57.7 %copy-start.2 = (bf16[2,2048,384]{2,1,0:T(8,128)(2,1)S(1)}, bf16[2,2048,384]{2,1,0:T(8,128)(2,1)}, u32[]{:S(2)}) copy-start(bf16[2,2048,384]{2,1,0:T(8,128)(2,1)} %param.23) | copy-start | bytes 9437188
  276.5 0.9 copy-start.1
  282.4 6.9 %copy-start.4 = (f32[2,8,8]{2,1,0:T(8,128)S(1)}, f32[2,8,8]{2,1,0:T(8,128)}, u32[]{:S(2)}) copy-start(f32[2,8,8]{2,1,0:T(8,128)} %param.22) | copy-start | bytes 1540
  285.0 20.9 %all-to-all-start.6 = ((bf16[2,16,5,2048]{3,0,2,1:T(2,128)(2,1)}), bf16[2,16,5,2048]{3,0,2,1:T(2,128)(2,1)}, u32[]{:S(2)}, u32[]{:S(2)}) async-start(bf16[2,16,5,2048]{3,0,2,1:T(2,128)(2,1)} %bitcast.81), calls=%async_computation.6 | async-start | bytes 1310720 | tf_op jit(solution)/shard_map/all_to_all | solution.py:112
